TPU v7x, 512 devices: a whole 4x8x8 slice. The times are simulated.
512 devices in a mesh: dom: 8 (over y_hi, core), fsdp: 64 (over x, z, y_lo).
Axes of the slice: x: 4, y: 8 (y_hi: 4, y_lo: 2; y = y_hi * 2 + y_lo), z: 8, core: 2. Of those that a mesh axis runs over, the one named last changes fastest.
Arguments:
- weights: bfloat16 [8, 64, 640, 896], P('dom', 'fsdp'), may hold values from -6 to 6
- activations: bfloat16 [8, 2, 1280, 2560], P('dom', None, 'fsdp'), may hold values from -6 to 6
- cotangents: bfloat16 [8, 2, 1280, 14336], P('dom', None, 'fsdp'), may hold values from -0.15625 to 0.15625
- lengths: int32 [8, 2, 64], P('dom', None, 'fsdp'), may hold values from 1 to 20, 960 in all within a row
Outputs:
- merged: bfloat16 [64, 640, 896], P('fsdp')
Inputs may be any that keep to these rules, and one draw needn't show every extreme that they name: In every domain and micro-batch the lengths sum to 960, and some block is full.
All inputs are finite; a program needn't handle non-finite values.
Results may differ from a plain program's by a relative error of at most 0.018.
Values may be sent and summed in bfloat16 or wider, within the bound.
No kernel may reach another device: no remote copies, remote signals or barrier semaphores. Data moves between devices by JAX's collectives and lax.ppermute only.
A program may use at most 64 MiB of HBM per device.

v0:
```python
import jax
import jax.numpy as jnp
from jax import lax
from jax.sharding import PartitionSpec as P

damping = 0.001


def squares(pieces):
    feat_rows, cot_rows = pieces
    grad = jnp.einsum("nmsr,nmsc->mrc", feat_rows, cot_rows, preferred_element_type=jnp.float32)
    return grad * grad


def body(weights, activations, cotangents, lengths):
    devices = lax.axis_size("fsdp")
    rows = weights.shape[2]
    cols = weights.shape[3]
    batches = activations.shape[1]
    slots = activations.shape[2]
    row_blocks = activations.shape[3] // rows
    col_blocks = devices // row_blocks
    mask = (jnp.arange(slots)[None, :] < lengths[0, :, 0:1]).astype(jnp.bfloat16)
    feats = activations[0] * mask[:, :, None]
    feat_blocks = feats.reshape(batches, slots, row_blocks, rows).transpose(2, 0, 1, 3)
    feat_send = jnp.broadcast_to(
        feat_blocks[:, None], (row_blocks, col_blocks, batches, slots, rows)
    ).reshape(devices, batches, slots, rows)
    cot_blocks = cotangents[0].reshape(batches, slots, col_blocks, cols).transpose(2, 0, 1, 3)
    cot_send = jnp.broadcast_to(
        cot_blocks[None], (row_blocks, col_blocks, batches, slots, cols)
    ).reshape(devices, batches, slots, cols)
    squared = squares(
        (
            lax.all_to_all(feat_send, "fsdp", split_axis=0, concat_axis=0, tiled=True),
            lax.all_to_all(cot_send, "fsdp", split_axis=0, concat_axis=0, tiled=True),
        )
    )
    fisher = jnp.sum(squared, axis=0) / batches
    term = fisher + damping
    numer_term = term * weights[0, 0].astype(jnp.float32)
    numer, denom = (
        lax.psum(numer_term.astype(jnp.bfloat16), "dom").astype(jnp.float32),
        lax.psum(term.astype(jnp.bfloat16), "dom").astype(jnp.float32),
    )
    merged = (numer / denom).astype(jnp.bfloat16)
    return merged[None]


def solution(mesh):
    return jax.shard_map(
        body,
        mesh=mesh,
        in_specs=(
            P("dom", "fsdp", None, None),
            P("dom", None, "fsdp", None),
            P("dom", None, "fsdp", None),
            P("dom", None, "fsdp"),
        ),
        out_specs=P("fsdp", None, None),
        check_vma=False,
    )
```

profile of v0, /device:TPU:21, one launch (start us, length us, event | category | flops | bytes accessed | tf_op | source)
XLA Modules:
  0.0 327.9 jit_solution(18246231903309940472)
XLA Ops:
  6.5 1.1 squeeze.2
  7.6 0.7 fusion.11
  8.3 0.2 multiply_bitcast_fusion
  8.4 0.2 copy.11
  8.6 3.4 %broadcast_in_dim.6 = bf16[4,16,2,20,640]{4,2,3,1,0:T(2,128)(2,1)} broadcast(bf16[4,2,20,640]{3,1,2,0:T(2,128)(2,1)S(1)} %copy.11), dimensions={0,2,3,4} | broadcast | bytes 3481600 | tf_op jit(solution)/shard_map/broadcast_in_dim | solution.py:26
  12.0 0.0 copy-start
  12.0 14.7 %all-to-all-start = ((bf16[64,2,20,640]{3,1,2,0:T(2,128)(2,1)}), bf16[64,2,20,640]{3,1,2,0:T(2,128)(2,1)}, u32[]{:S(2)}, u32[]{:S(2)}) async-start(bf16[64,2,20,640]{3,1,2,0:T(2,128)(2,1)} %bitcast.2), calls=%async_computation | async-start | bytes 6553600 | tf_op jit(solution)/shard_map/all_to_all | solution.py:35
  26.7 0.0 all-reduce.3.cloned.1.call-start
  26.7 0.0 copy-done
  26.7 0.8 reshape_squeeze.3
  27.5 0.9 copy.12
  28.4 70.2 %all-to-all-done = bf16[64,2,20,640]{3,1,2,0:T(2,128)(2,1)} async-done(((bf16[64,2,20,640]{3,1,2,0:T(2,128)(2,1)}), bf16[64,2,20,640]{3,1,2,0:T(2,128)(2,1)}, u32[]{:S(2)}, u32[]{:S(2)}) %all-to-all-start) | async-done | bytes 3276832 | tf_op jit(solution)/shard_map/all_to_all | solution.py:35
  98.6 4.4 %broadcast_in_dim.7 = bf16[4,16,2,20,896]{4,2,3,1,0:T(2,128)(2,1)} broadcast(bf16[16,2,20,896]{3,1,2,0:T(2,128)(2,1)S(1)} %copy.12), dimensions={1,2,3,4} | broadcast | bytes 5734400 | tf_op jit(solution)/shard_map/broadcast_in_dim | solution.py:30
  103.1 114.3 %all_to_all.10 = bf16[64,2,20,896]{3,1,2,0:T(2,128)(2,1)S(1)} all-to-all(bf16[64,2,20,896]{3,1,2,0:T(2,128)(2,1)} %bitcast.20), channel_id=1, replica_groups=mesh['dom'=8,'fsdp'=64] {'fsdp'}, dimensions={0} | all-to-all | bytes 9175040 | tf_op jit(solution)/shard_map/all_to_all | solution.py:36
  217.3 0.0 copy-start.1
  217.3 5.8 %fusion = f32[640,896]{1,0:T(8,128)S(1)} fusion(bf16[64,2,20,896]{3,1,2,0:T(2,128)(2,1)S(1)} %all_to_all.10, bf16[64,2,20,640]{3,1,2,0:T(2,128)(2,1)} %all-to-all-done), kind=kOutput, calls=%fused_computation.1 | convolution fusion | flops 2937733120 | bytes 10158080 | tf_op jit(solution)/shard_map/nmsr,nmsc->mrc/dot_general | solution.py:11
  223.2 0.0 copy-done.1
  223.2 1.8 fusion.4
  225.0 0.0 all-reduce.3.cloned.1.call-update
  225.0 93.1 %all-reduce.3.cloned.1.call-done = (bf16[640,896]{1,0:T(8,128)(2,1)}, bf16[640,896]{1,0:T(8,128)(2,1)}) async-done(((bf16[640,896]{1,0:T(8,128)(2,1)}, bf16[640,896]{1,0:T(8,128)(2,1)}), (bf16[640,896]{1,0:T(8,128)(2,1)}, bf16[640,896]{1,0:T(8,128)(2,1)})) %all-reduce.3.cloned.1.call-update) | async-done | bytes 2293776 | tf_op jit(solution)/shard_map/psum | solution.py:44
  318.1 3.0 fusion.10
Async XLA Ops:
  12.0 14.7 %copy-start = (bf16[1,2,20,14336]{3,1,2,0:T(2,128)(2,1)S(1)}, bf16[1,2,20,14336]{3,1,2,0:T(2,128)(2,1)}, u32[]{:S(2)}) copy-start(bf16[1,2,20,14336]{3,1,2,0:T(2,128)(2,1)} %param.6) | copy-start | bytes 3440644
  12.0 86.7 %all-to-all-start = ((bf16[64,2,20,640]{3,1,2,0:T(2,128)(2,1)}), bf16[64,2,20,640]{3,1,2,0:T(2,128)(2,1)}, u32[]{:S(2)}, u32[]{:S(2)}) async-start(bf16[64,2,20,640]{3,1,2,0:T(2,128)(2,1)} %bitcast.2), calls=%async_computation | async-start | bytes 6553600 | tf_op jit(solution)/shard_map/all_to_all | solution.py:35
  26.7 291.4 %all-reduce.3.cloned.1.call-start = ((), (), s32[]{:S(2)}) async-start(), calls=%async_computation.2 | async-start | bytes 4587520 | tf_op jit(solution)/shard_map/psum | solution.py:44
  217.3 5.9 %copy-start.1 = (bf16[1,1,640,896]{3,2,1,0:T(8,128)(2,1)S(1)}, bf16[1,1,640,896]{3,2,1,0:T(8,128)(2,1)}, u32[]{:S(2)}) copy-start(bf16[1,1,640,896]{3,2,1,0:T(8,128)(2,1)} %param.4) | copy-start | bytes 3440644
Sparse Core Ops, SparseCore 0:
  225.1 92.9 all-reduce.2
where the time goes:
time: 328 us
  waiting for transfers between devices  163 us (50%)
  blocking collectives  114 us (35%)
  starting transfers between devices  14.7 us (4%)
  between operations  13.5 us (4%)
  local copies, waits for them, and re-layouts  10.7 us (3%)
  matrix products  5.84 us (2%)
  other arithmetic  5.63 us (2%)
    all_to_all x1, blocking collectives, body(): lax.all_to_all(cot_send, 'fsdp', split_axis=0, concat_axis=0, tiled=True)  114 us
    psum x1, waiting for transfers between devices, body(): lax.psum(term.astype(jnp.bfloat16), 'dom').astype(jnp.float32)  93.1 us
    all_to_all x1, waiting for transfers between devices, body(): lax.all_to_all(feat_send, 'fsdp', split_axis=0, concat_axis=0, tiled=True)  70.2 us
    all_to_all x1, starting transfers between devices, body(): lax.all_to_all(feat_send, 'fsdp', split_axis=0, concat_axis=0, tiled=True)  14.7 us
  transfers between devices with their start and end apart: 2, of which 2 were waited for; matrix products, arithmetic and copies ran while one was open for 1% of the time, Pallas kernels for 0%

commit v1 on v0

v1 whole, which is shorter than its diff:
```python
import jax
import jax.numpy as jnp
from jax import lax
from jax.sharding import Mesh, PartitionSpec as P

damping = 0.001
axes = ("yhi", "core", "x", "z", "ylo")


def shift(value, axis, by):
    count = lax.axis_size(axis)
    return lax.ppermute(value, axis, [(i, (i + by) % count) for i in range(count)])


def exchange(value, axis):
    return lax.all_to_all(value, axis, split_axis=0, concat_axis=0, tiled=True)


def put(whole, piece, dim, index, split=None, start=0):
    at = [0] * whole.ndim
    at[dim] = index % whole.shape[dim]
    if split is not None:
        at[split] = start
    return lax.dynamic_update_slice(whole, jnp.expand_dims(piece, dim), at)


def room(own, axis, dim):
    shape = list(own.shape)
    shape.insert(dim, lax.axis_size(axis))
    return jnp.zeros(shape, own.dtype)


def body(weights, activations, cotangents, lengths):
    xs, zs, ys = (lax.axis_size(a) for a in ("x", "z", "ylo"))
    cores, his = lax.axis_size("core"), lax.axis_size("yhi")
    x, z, y, core = (lax.axis_index(a) for a in ("x", "z", "ylo", "core"))
    rows, cols = weights.shape[2:]
    batches, slots = activations.shape[1:3]

    cots = cotangents[0].reshape(batches, slots, zs * ys, cols).transpose(2, 0, 1, 3)
    cots = exchange(cots, ("z", "ylo"))
    cots = cots.reshape(zs, ys, batches, slots, cols).transpose(2, 0, 1, 3, 4).reshape(batches, zs, ys * slots, cols)

    mask = (jnp.arange(slots)[None, :] < lengths[0, :, 0:1]).astype(jnp.bfloat16)
    feats = (activations[0] * mask[:, :, None]).reshape(batches, slots, xs, rows).transpose(2, 0, 1, 3)
    own = lax.dynamic_index_in_dim(feats, x, 0, keepdims=False)
    plane = put(room(own, "x", 1), own, 1, x)
    for k in range(1, xs):
        block = lax.dynamic_index_in_dim(feats, (x + k) % xs, 0, keepdims=False)
        plane = put(plane, shift(block, "x", k), 1, x - k)
    pair = put(room(plane, "ylo", 2), plane, 2, y)
    pair = put(pair, shift(plane, "ylo", 1), 2, 1 - y)
    own = pair.reshape(batches, xs * ys * slots, rows)

    whole = put(room(own, "z", 1), own, 1, z)
    up = down = own
    for k in range(1, zs // 2):
        up, down = shift(up, "z", 1), shift(down, "z", -1)
        whole = put(put(whole, up, 1, z - k), down, 1, z + k)
    down = shift(down, "z", -1)
    feats = put(whole, down, 1, z + zs // 2).reshape(batches, -1, rows)

    whole = put(room(cots, "x", 2), cots, 2, x)
    up, down = shift(cots, "x", 1), shift(cots, "x", -1)
    whole = put(put(whole, up, 2, x - 1), down, 2, x + 1)
    half = zs // 2
    up, down = shift(up[:, :half], "x", 1), shift(down[:, half:], "x", -1)
    whole = put(put(whole, up, 2, x + 2), down, 2, x + 2, 1, half)
    cots = whole.reshape(batches, -1, cols)

    grad = jnp.einsum("mkr,mkc->mrc", feats, cots, preferred_element_type=jnp.float32)
    term = jnp.sum(grad * grad, axis=0) / batches + damping
    numer = (term * weights[0, 0].astype(jnp.float32)).astype(jnp.bfloat16)
    terms = jnp.stack([numer, term.astype(jnp.bfloat16)])
    terms = terms.reshape(2, cores, his, rows // cores // his, cols)
    other = shift(lax.dynamic_index_in_dim(terms, 1 - core, 1, keepdims=False), "core", 1)
    mine = lax.dynamic_index_in_dim(terms, core, 1, keepdims=False)
    both = (mine.astype(jnp.float32) + other.astype(jnp.float32)).astype(jnp.bfloat16)
    both = exchange(both.transpose(1, 0, 2, 3), "yhi")
    sums = jnp.sum(both.astype(jnp.float32), axis=0)
    merged = (sums[0] / sums[1]).astype(jnp.bfloat16)
    merged = exchange(jnp.broadcast_to(merged[None], (his,) + merged.shape), "yhi")
    merged = merged.reshape(rows // cores, cols)
    other = shift(merged, "core", 1)
    out = jnp.where(core == 0, jnp.stack([merged, other]), jnp.stack([other, merged]))
    return out.reshape(1, rows, cols)


def solution(mesh):
    inner = Mesh(mesh.devices.reshape(4, 2, 4, 8, 2), axes)
    dom, fsdp = axes[:2], axes[2:]
    return jax.shard_map(
        body,
        mesh=inner,
        in_specs=(
            P(dom, fsdp, None, None),
            P(dom, None, fsdp, None),
            P(dom, None, fsdp, None),
            P(dom, None, fsdp),
        ),
        out_specs=P(fsdp, None, None),
        check_vma=False,
    )
```

time: 328 us -> 193 us (0.59)
  the two profiles are of different devices: /device:TPU:21 before, /device:TPU:15 now
where the time goes in v1:
time: 193 us; the launch traced here: 192 us
  starting transfers between devices  67.8 us (35%)
  blocking collectives  52.3 us (27%)
  waiting for transfers between devices  49.7 us (26%)
  local copies, waits for them, and re-layouts  13.7 us (7%)
  matrix products  4.16 us (2%)
  other arithmetic  3.65 us (2%)
    ppermute x17, starting transfers between devices, shift(): lax.ppermute(value, axis, [(i, (i + by) % count) for i in range(count)])  56.5 us
    all_to_all x2, blocking collectives, exchange(): return lax.all_to_all(value, axis, split_axis=0, concat_axis=0, tiled=True)  52.3 us
    ppermute x17, waiting for transfers between devices, shift(): lax.ppermute(value, axis, [(i, (i + by) % count) for i in range(count)])  49.7 us
    all_to_all x1, starting transfers between devices, exchange(): return lax.all_to_all(value, axis, split_axis=0, concat_axis=0, tiled=True)  11.2 us
    dynamic_update_slice x19, local copies, waits for them, and re-layouts, put(): return lax.dynamic_update_slice(whole, jnp.expand_dims(piece, dim), at)  5.66 us
    another operation x2, local copies, waits for them, and re-layouts, body(): cotangents[0].reshape(batches, slots, zs * ys, cols).transpose(2, 0, 1, 3)  4.97 us
    dot_general x1, matrix products, body(): jnp.einsum('mkr,mkc->mrc', feats, cots, preferred_element_type=jnp.float32)  4.16 us
  transfers between devices with their start and end apart: 18, of which 11 were waited for; matrix products, arithmetic and copies ran while one was open for 4% of the time, Pallas kernels for 0%

profile of v1, /device:TPU:15, one launch (start us, length us, event | category | flops | bytes accessed | tf_op | source)
XLA Modules:
  0.0 192.0 jit_solution(13083945613423585589)
XLA Ops:
  0.0 3.1 %reshape_squeeze.3 = bf16[2,20,16,896]{3,2,0,1:T(8,128)(2,1)S(1)} reshape(bf16[1,2,20,14336]{3,1,2,0:T(2,128)(2,1)} %param.6) | data formatting | bytes 2293760 | tf_op jit(solution)/shard_map/reshape;squeeze | solution.py:40
  3.1 1.9 copy.99
  5.0 11.2 %all-to-all-start = ((bf16[16,2,20,896]{3,1,2,0:T(2,128)(2,1)}), bf16[16,2,20,896]{3,1,2,0:T(2,128)(2,1)S(1)}, u32[]{:S(2)}, u32[]{:S(2)}) async-start(bf16[16,2,20,896]{3,1,2,0:T(2,128)(2,1)} %bitcast.68), calls=%async_computation | async-start | bytes 2293760 | tf_op jit(solution)/shard_map/all_to_all | solution.py:16
  16.2 0.1 squeeze.23
  16.4 0.3 copy_multiply_fusion
  16.7 0.1 dynamic-slice_bitcast_fusion
  16.8 2.1 %collective-permute-start = (bf16[2,20,640]{2,0,1:T(2,128)(2,1)S(1)}, bf16[2,20,640]{2,0,1:T(2,128)(2,1)S(1)}, u32[]{:S(2)}, u32[]{:S(2)}) collective-permute-start(bf16[2,20,640]{2,0,1:T(2,128)(2,1)S(1)} %get-tuple-element.7), channel_id=1, source_target_pairs={{0,16},{16,32},{32,48},{48,0},{1,17},{17,33},{33,49},{49,1},{2,18}... | collective-permute-start | bytes 153608 | tf_op jit(solution)/shard_map/ppermute | solution.py:12
  18.9 4.0 %collective-permute-start.1 = (bf16[2,20,640]{2,0,1:T(2,128)(2,1)S(1)}, bf16[2,20,640]{2,0,1:T(2,128)(2,1)S(1)}, u32[]{:S(2)}, u32[]{:S(2)}) collective-permute-start(bf16[2,20,640]{2,0,1:T(2,128)(2,1)S(1)} %get-tuple-element.6), channel_id=1, source_target_pairs={{0,32},{16,48},{32,0},{48,16},{1,33},{17,49},{33,1},{49,17},{2,34}... | collective-permute-start | bytes 153608 | tf_op jit(solution)/shard_map/ppermute | solution.py:12
  23.0 1.9 %collective-permute-start.2 = (bf16[2,20,640]{2,0,1:T(2,128)(2,1)S(1)}, bf16[2,20,640]{2,0,1:T(2,128)(2,1)S(1)}, u32[]{:S(2)}, u32[]{:S(2)}) collective-permute-start(bf16[2,20,640]{2,0,1:T(2,128)(2,1)S(1)} %get-tuple-element.5), channel_id=1, source_target_pairs={{0,48},{16,0},{32,16},{48,32},{1,49},{17,1},{33,17},{49,33},{2,50}... | collective-permute-start | bytes 153608 | tf_op jit(solution)/shard_map/ppermute | solution.py:12
  24.9 0.1 broadcast_in_dim.75
  25.2 0.2 collective-permute-done.1
  25.5 3.9 %collective-permute-done.2 = bf16[2,20,640]{2,0,1:T(2,128)(2,1)S(1)} collective-permute-done((bf16[2,20,640]{2,0,1:T(2,128)(2,1)S(1)}, bf16[2,20,640]{2,0,1:T(2,128)(2,1)S(1)}, u32[]{:S(2)}, u32[]{:S(2)}) %collective-permute-start.2) | collective-permute-done | bytes 51232 | tf_op jit(solution)/shard_map/ppermute | solution.py:12
  29.4 2.1 %collective-permute-start.3 = (bf16[2,4,20,640]{3,0,2,1:T(2,128)(2,1)S(1)}, bf16[2,4,20,640]{3,0,2,1:T(2,128)(2,1)S(1)}, u32[]{:S(2)}, u32[]{:S(2)}) collective-permute-start(bf16[2,4,20,640]{3,0,2,1:T(2,128)(2,1)S(1)} %bitcast_dynamic-update-slice_fusion.2), channel_id=1, source_target_pairs={{0,1},{1,0},{2,3},{3,2},{4,5},{5,4},{6,7},{7,6},{8,9},{9,8},{10,11... | collective-permute-start | bytes 614408 | tf_op jit(solution)/shard_map/ppermute | solution.py:12
  31.4 0.2 broadcast_in_dim.74
  31.7 0.2 bitcast_dynamic-update-slice_fusion.1
  31.8 7.2 %collective-permute-done.3 = bf16[2,4,20,640]{3,0,2,1:T(2,128)(2,1)S(1)} collective-permute-done((bf16[2,4,20,640]{3,0,2,1:T(2,128)(2,1)S(1)}, bf16[2,4,20,640]{3,0,2,1:T(2,128)(2,1)S(1)}, u32[]{:S(2)}, u32[]{:S(2)}) %collective-permute-start.3) | collective-permute-done | bytes 204832 | tf_op jit(solution)/shard_map/ppermute | solution.py:12
  39.1 0.2 bitcast_dynamic-update-slice_fusion
  39.3 2.3 %collective-permute-start.4 = (bf16[2,160,640]{2,0,1:T(2,128)(2,1)S(1)}, bf16[2,160,640]{2,0,1:T(2,128)(2,1)S(1)}, u32[]{:S(2)}, u32[]{:S(2)}) collective-permute-start(bf16[2,160,640]{2,0,1:T(2,128)(2,1)S(1)} %bitcast.79), channel_id=1, source_target_pairs={{0,2},{2,4},{4,6},{6,8},{8,10},{10,12},{12,14},{14,0},{1,3},{3,5},... | collective-permute-start | bytes 1228808 | tf_op jit(solution)/shard_map/ppermute | solution.py:12
  41.6 4.2 %collective-permute-start.5 = (bf16[2,160,640]{2,0,1:T(2,128)(2,1)S(1)}, bf16[2,160,640]{2,0,1:T(2,128)(2,1)S(1)}, u32[]{:S(2)}, u32[]{:S(2)}) collective-permute-start(bf16[2,160,640]{2,0,1:T(2,128)(2,1)S(1)} %bitcast.80), channel_id=1, source_target_pairs={{0,14},{2,0},{4,2},{6,4},{8,6},{10,8},{12,10},{14,12},{1,15},{3,1}... | collective-permute-start | bytes 1228808 | tf_op jit(solution)/shard_map/ppermute | solution.py:12
  45.9 0.3 broadcast_in_dim.73
  46.3 6.4 %collective-permute-done.4 = bf16[2,160,640]{2,0,1:T(2,128)(2,1)S(1)} collective-permute-done((bf16[2,160,640]{2,0,1:T(2,128)(2,1)S(1)}, bf16[2,160,640]{2,0,1:T(2,128)(2,1)S(1)}, u32[]{:S(2)}, u32[]{:S(2)}) %collective-permute-start.4) | collective-permute-done | bytes 409632 | tf_op jit(solution)/shard_map/ppermute | solution.py:12
  52.7 1.9 collective-permute-start.6
  54.6 4.6 %collective-permute-start.7 = (bf16[2,160,640]{2,0,1:T(2,128)(2,1)S(1)}, bf16[2,160,640]{2,0,1:T(2,128)(2,1)S(1)}, u32[]{:S(2)}, u32[]{:S(2)}) collective-permute-start(bf16[2,160,640]{2,0,1:T(2,128)(2,1)S(1)} %collective-permute-done.5), channel_id=1, source_target_pairs={{0,14},{2,0},{4,2},{6,4},{8,6},{10,8},{12,10},{14,12},{1,15},{3,1}... | collective-permute-start | bytes 1228808 | tf_op jit(solution)/shard_map/ppermute | solution.py:12
  59.3 5.4 %collective-permute-done.6 = bf16[2,160,640]{2,0,1:T(2,128)(2,1)S(1)} collective-permute-done((bf16[2,160,640]{2,0,1:T(2,128)(2,1)S(1)}, bf16[2,160,640]{2,0,1:T(2,128)(2,1)S(1)}, u32[]{:S(2)}, u32[]{:S(2)}) %collective-permute-start.6) | collective-permute-done | bytes 409632 | tf_op jit(solution)/shard_map/ppermute | solution.py:12
  64.8 1.9 collective-permute-start.8
  66.7 4.6 %collective-permute-start.9 = (bf16[2,160,640]{2,0,1:T(2,128)(2,1)S(1)}, bf16[2,160,640]{2,0,1:T(2,128)(2,1)S(1)}, u32[]{:S(2)}, u32[]{:S(2)}) collective-permute-start(bf16[2,160,640]{2,0,1:T(2,128)(2,1)S(1)} %collective-permute-done.7), channel_id=1, source_target_pairs={{0,14},{2,0},{4,2},{6,4},{8,6},{10,8},{12,10},{14,12},{1,15},{3,1}... | collective-permute-start | bytes 1228808 | tf_op jit(solution)/shard_map/ppermute | solution.py:12
  71.3 0.2 copy.71
  71.5 1.9 %collective-permute-start.11 = (bf16[2,8,40,896]{3,1,2,0:T(8,128)(2,1)S(1)}, bf16[2,8,40,896]{3,1,2,0:T(8,128)(2,1)S(1)}, u32[]{:S(2)}, u32[]{:S(2)}) collective-permute-start(bf16[2,8,40,896]{3,1,2,0:T(8,128)(2,1)S(1)} %bitcast.83), channel_id=1, source_target_pairs={{0,16},{16,32},{32,48},{48,0},{1,17},{17,33},{33,49},{49,1},{2,18}... | collective-permute-start | bytes 3440648 | tf_op jit(solution)/shard_map/ppermute | solution.py:12
  73.4 0.8 copy_dynamic-update-slice_fusion.9
  74.3 3.4 %collective-permute-start.12 = (bf16[2,8,40,896]{3,1,2,0:T(8,128)(2,1)S(1)}, bf16[2,8,40,896]{3,1,2,0:T(8,128)(2,1)S(1)}, u32[]{:S(2)}, u32[]{:S(2)}) collective-permute-start(bf16[2,8,40,896]{3,1,2,0:T(8,128)(2,1)S(1)} %bitcast.84), channel_id=1, source_target_pairs={{0,48},{16,0},{32,16},{48,32},{1,49},{17,1},{33,17},{49,33},{2,50}... | collective-permute-start | bytes 3440648 | tf_op jit(solution)/shard_map/ppermute | solution.py:12
  77.6 0.8 copy_dynamic-update-slice_fusion.8
  78.4 3.8 %collective-permute-start.10 = (bf16[2,160,640]{2,0,1:T(2,128)(2,1)S(1)}, bf16[2,160,640]{2,0,1:T(2,128)(2,1)S(1)}, u32[]{:S(2)}, u32[]{:S(2)}) collective-permute-start(bf16[2,160,640]{2,0,1:T(2,128)(2,1)S(1)} %collective-permute-done.9), channel_id=1, source_target_pairs={{0,14},{2,0},{4,2},{6,4},{8,6},{10,8},{12,10},{14,12},{1,15},{3,1}... | collective-permute-start | bytes 1228808 | tf_op jit(solution)/shard_map/ppermute | solution.py:12
  82.2 0.8 copy_dynamic-update-slice_fusion.7
  83.1 0.8 copy_dynamic-update-slice_fusion.6
  83.9 3.5 %collective-permute-done.10 = bf16[2,160,640]{2,0,1:T(2,128)(2,1)S(1)} collective-permute-done((bf16[2,160,640]{2,0,1:T(2,128)(2,1)S(1)}, bf16[2,160,640]{2,0,1:T(2,128)(2,1)S(1)}, u32[]{:S(2)}, u32[]{:S(2)}) %collective-permute-start.10) | collective-permute-done | bytes 409632 | tf_op jit(solution)/shard_map/ppermute | solution.py:12
  87.4 0.8 copy_dynamic-update-slice_fusion.5
  88.2 8.6 %collective-permute-done.11 = bf16[2,8,40,896]{3,1,2,0:T(8,128)(2,1)S(1)} collective-permute-done((bf16[2,8,40,896]{3,1,2,0:T(8,128)(2,1)S(1)}, bf16[2,8,40,896]{3,1,2,0:T(8,128)(2,1)S(1)}, u32[]{:S(2)}, u32[]{:S(2)}) %collective-permute-start.11) | collective-permute-done | bytes 1146912 | tf_op jit(solution)/shard_map/ppermute | solution.py:12
  96.8 0.2 slice.16
  96.9 3.1 %collective-permute-start.13 = (bf16[2,4,40,896]{3,1,2,0:T(4,128)(2,1)S(1)}, bf16[2,4,40,896]{3,1,2,0:T(4,128)(2,1)S(1)}, u32[]{:S(2)}, u32[]{:S(2)}) collective-permute-start(bf16[2,4,40,896]{3,1,2,0:T(4,128)(2,1)S(1)} %slice.16), channel_id=1, source_target_pairs={{0,16},{16,32},{32,48},{48,0},{1,17},{17,33},{33,49},{49,1},{2,18}... | collective-permute-start | bytes 1720328 | tf_op jit(solution)/shard_map/ppermute | solution.py:12
  100.0 0.4 broadcast_in_dim.89
  100.4 0.2 copy_dynamic-update-slice_fusion
  100.7 0.3 slice.17
  101.0 2.2 %collective-permute-start.14 = (bf16[2,4,40,896]{3,1,2,0:T(4,128)(2,1)S(1)}, bf16[2,4,40,896]{3,1,2,0:T(4,128)(2,1)S(1)}, u32[]{:S(2)}, u32[]{:S(2)}) collective-permute-start(bf16[2,4,40,896]{3,1,2,0:T(4,128)(2,1)S(1)} %slice.17), channel_id=1, source_target_pairs={{0,48},{16,0},{32,16},{48,32},{1,49},{17,1},{33,17},{49,33},{2,50}... | collective-permute-start | bytes 1720328 | tf_op jit(solution)/shard_map/ppermute | solution.py:12
  103.2 0.2 copy_dynamic-update-slice_fusion.2
  103.4 0.2 copy_dynamic-update-slice_fusion.1
  103.6 5.4 %collective-permute-done.13 = bf16[2,4,40,896]{3,1,2,0:T(4,128)(2,1)S(1)} collective-permute-done((bf16[2,4,40,896]{3,1,2,0:T(4,128)(2,1)S(1)}, bf16[2,4,40,896]{3,1,2,0:T(4,128)(2,1)S(1)}, u32[]{:S(2)}, u32[]{:S(2)}) %collective-permute-start.13) | collective-permute-done | bytes 573472 | tf_op jit(solution)/shard_map/ppermute | solution.py:12
  109.1 0.1 copy_dynamic-update-slice_fusion.4
  109.2 4.8 %collective-permute-done.14 = bf16[2,4,40,896]{3,1,2,0:T(4,128)(2,1)S(1)} collective-permute-done((bf16[2,4,40,896]{3,1,2,0:T(4,128)(2,1)S(1)}, bf16[2,4,40,896]{3,1,2,0:T(4,128)(2,1)S(1)}, u32[]{:S(2)}, u32[]{:S(2)}) %collective-permute-start.14) | collective-permute-done | bytes 573472 | tf_op jit(solution)/shard_map/ppermute | solution.py:12
  114.0 0.1 copy_dynamic-update-slice_fusion.3
  114.1 4.2 %multiply_reduce_fusion = f32[640,896]{1,0:T(8,128)S(1)} fusion(bf16[2,1280,640]{2,1,0:T(8,128)(2,1)S(1)} %bitcast.74, bf16[2,1280,896]{2,1,0:T(8,128)(2,1)S(1)} %bitcast.73), kind=kOutput, calls=%fused_computation | convolution fusion | flops 2937733120 | bytes 10158080 | tf_op jit(solution)/shard_map/mkr,mkc->mrc/dot_general | solution.py:71
  118.3 0.2 multiply_add_fusion
  118.5 0.1 convert_element_type.66
  118.7 1.1 copy-done.2
  119.8 0.2 fusion.1
  120.0 1.1 fusion.4
  121.2 7.4 %collective-permute-start.15 = (bf16[2,4,80,896]{3,2,0,1:T(8,128)(2,1)}, bf16[2,4,80,896]{3,2,0,1:T(8,128)(2,1)S(1)}, u32[]{:S(2)}, u32[]{:S(2)}) collective-permute-start(bf16[2,4,80,896]{3,2,0,1:T(8,128)(2,1)} %fusion.4), channel_id=1, source_target_pairs={{0,64},{64,0},{1,65},{65,1},{2,66},{66,2},{3,67},{67,3},{4,68},{68... | collective-permute-start | bytes 3440648 | tf_op jit(solution)/shard_map/ppermute | solution.py:12
  128.5 2.6 %collective-permute-done.15 = bf16[2,4,80,896]{3,2,0,1:T(8,128)(2,1)S(1)} collective-permute-done((bf16[2,4,80,896]{3,2,0,1:T(8,128)(2,1)}, bf16[2,4,80,896]{3,2,0,1:T(8,128)(2,1)S(1)}, u32[]{:S(2)}, u32[]{:S(2)}) %collective-permute-start.15) | collective-permute-done | bytes 1146912 | tf_op jit(solution)/shard_map/ppermute | solution.py:12
  131.1 0.3 fusion.2
  131.4 34.9 %all_to_all.15 = bf16[4,2,80,896]{3,2,1,0:T(8,128)(2,1)S(1)} all-to-all(bf16[4,2,80,896]{3,2,1,0:T(8,128)(2,1)S(1)} %fusion.2), channel_id=1, replica_groups=mesh['yhi'=4,'core'=2,'x'=4,'z'=8,'ylo'=2] {'yhi'}, dimensions={0} | all-to-all | bytes 2293760 | tf_op jit(solution)/shard_map/all_to_all | solution.py:16
  166.3 0.1 convert_reduce_fusion
  166.6 17.4 %all_to_all.16 = bf16[4,80,896]{2,1,0:T(8,128)(2,1)S(1)} all-to-all(bf16[4,80,896]{2,1,0:T(8,128)(2,1)S(1)} %broadcast_in_dim.95), channel_id=1, replica_groups=mesh['yhi'=4,'core'=2,'x'=4,'z'=8,'ylo'=2] {'yhi'}, dimensions={0} | all-to-all | bytes 1146880 | tf_op jit(solution)/shard_map/all_to_all | solution.py:16
  184.0 5.2 %collective-permute-start.16 = (bf16[320,896]{1,0:T(8,128)(2,1)S(1)}, bf16[320,896]{1,0:T(8,128)(2,1)S(1)}, u32[]{:S(2)}, u32[]{:S(2)}) collective-permute-start(bf16[320,896]{1,0:T(8,128)(2,1)S(1)} %bitcast.77), channel_id=1, source_target_pairs={{0,64},{64,0},{1,65},{65,1},{2,66},{66,2},{3,67},{67,3},{4,68},{68... | collective-permute-start | bytes 1720328 | tf_op jit(solution)/shard_map/ppermute | solution.py:12
  189.2 1.6 collective-permute-done.16
  190.8 1.2 maximum_select_fusion
  (26 shorter events, 0.6 us)
Async XLA Ops:
  3.1 13.1 %copy-start.3 = (bf16[1,2,20,2560]{3,1,2,0:T(2,128)(2,1)S(1)}, bf16[1,2,20,2560]{3,1,2,0:T(2,128)(2,1)}, u32[]{:S(2)}) copy-start(bf16[1,2,20,2560]{3,1,2,0:T(2,128)(2,1)} %param.5) | copy-start | bytes 614404
  3.1 13.3 %copy-start.4 = (s32[1,2,1]{1,2,0:T(1,128)S(1)}, s32[1,2,1]{1,2,0:T(1,128)}, u32[]{:S(2)}) copy-start(s32[1,2,1]{1,2,0:T(1,128)} %param.7) | copy-start | bytes 28
  5.0 66.3 %all-to-all-start = ((bf16[16,2,20,896]{3,1,2,0:T(2,128)(2,1)}), bf16[16,2,20,896]{3,1,2,0:T(2,128)(2,1)S(1)}, u32[]{:S(2)}, u32[]{:S(2)}) async-start(bf16[16,2,20,896]{3,1,2,0:T(2,128)(2,1)} %bitcast.68), calls=%async_computation | async-start | bytes 2293760 | tf_op jit(solution)/shard_map/all_to_all | solution.py:16
  16.8 8.4 %collective-permute-start = (bf16[2,20,640]{2,0,1:T(2,128)(2,1)S(1)}, bf16[2,20,640]{2,0,1:T(2,128)(2,1)S(1)}, u32[]{:S(2)}, u32[]{:S(2)}) collective-permute-start(bf16[2,20,640]{2,0,1:T(2,128)(2,1)S(1)} %get-tuple-element.7), channel_id=1, source_target_pairs={{0,16},{16,32},{32,48},{48,0},{1,17},{17,33},{33,49},{49,1},{2,18}... | collective-permute-start | bytes 153608 | tf_op jit(solution)/shard_map/ppermute | solution.py:12
  18.9 6.5 %collective-permute-start.1 = (bf16[2,20,640]{2,0,1:T(2,128)(2,1)S(1)}, bf16[2,20,640]{2,0,1:T(2,128)(2,1)S(1)}, u32[]{:S(2)}, u32[]{:S(2)}) collective-permute-start(bf16[2,20,640]{2,0,1:T(2,128)(2,1)S(1)} %get-tuple-element.6), channel_id=1, source_target_pairs={{0,32},{16,48},{32,0},{48,16},{1,33},{17,49},{33,1},{49,17},{2,34}... | collective-permute-start | bytes 153608 | tf_op jit(solution)/shard_map/ppermute | solution.py:12
  23.0 6.4 %collective-permute-start.2 = (bf16[2,20,640]{2,0,1:T(2,128)(2,1)S(1)}, bf16[2,20,640]{2,0,1:T(2,128)(2,1)S(1)}, u32[]{:S(2)}, u32[]{:S(2)}) collective-permute-start(bf16[2,20,640]{2,0,1:T(2,128)(2,1)S(1)} %get-tuple-element.5), channel_id=1, source_target_pairs={{0,48},{16,0},{32,16},{48,32},{1,49},{17,1},{33,17},{49,33},{2,50}... | collective-permute-start | bytes 153608 | tf_op jit(solution)/shard_map/ppermute | solution.py:12
  29.4 9.7 %collective-permute-start.3 = (bf16[2,4,20,640]{3,0,2,1:T(2,128)(2,1)S(1)}, bf16[2,4,20,640]{3,0,2,1:T(2,128)(2,1)S(1)}, u32[]{:S(2)}, u32[]{:S(2)}) collective-permute-start(bf16[2,4,20,640]{3,0,2,1:T(2,128)(2,1)S(1)} %bitcast_dynamic-update-slice_fusion.2), channel_id=1, source_target_pairs={{0,1},{1,0},{2,3},{3,2},{4,5},{5,4},{6,7},{7,6},{8,9},{9,8},{10,11... | collective-permute-start | bytes 614408 | tf_op jit(solution)/shard_map/ppermute | solution.py:12
  39.3 13.4 %collective-permute-start.4 = (bf16[2,160,640]{2,0,1:T(2,128)(2,1)S(1)}, bf16[2,160,640]{2,0,1:T(2,128)(2,1)S(1)}, u32[]{:S(2)}, u32[]{:S(2)}) collective-permute-start(bf16[2,160,640]{2,0,1:T(2,128)(2,1)S(1)} %bitcast.79), channel_id=1, source_target_pairs={{0,2},{2,4},{4,6},{6,8},{8,10},{10,12},{12,14},{14,0},{1,3},{3,5},... | collective-permute-start | bytes 1228808 | tf_op jit(solution)/shard_map/ppermute | solution.py:12
  41.6 13.0 %collective-permute-start.5 = (bf16[2,160,640]{2,0,1:T(2,128)(2,1)S(1)}, bf16[2,160,640]{2,0,1:T(2,128)(2,1)S(1)}, u32[]{:S(2)}, u32[]{:S(2)}) collective-permute-start(bf16[2,160,640]{2,0,1:T(2,128)(2,1)S(1)} %bitcast.80), channel_id=1, source_target_pairs={{0,14},{2,0},{4,2},{6,4},{8,6},{10,8},{12,10},{14,12},{1,15},{3,1}... | collective-permute-start | bytes 1228808 | tf_op jit(solution)/shard_map/ppermute | solution.py:12
  52.7 12.1 %collective-permute-start.6 = (bf16[2,160,640]{2,0,1:T(2,128)(2,1)S(1)}, bf16[2,160,640]{2,0,1:T(2,128)(2,1)S(1)}, u32[]{:S(2)}, u32[]{:S(2)}) collective-permute-start(bf16[2,160,640]{2,0,1:T(2,128)(2,1)S(1)} %collective-permute-done.4), channel_id=1, source_target_pairs={{0,2},{2,4},{4,6},{6,8},{8,10},{10,12},{12,14},{14,0},{1,3},{3,5},... | collective-permute-start | bytes 1228808 | tf_op jit(solution)/shard_map/ppermute | solution.py:12
  54.6 12.1 %collective-permute-start.7 = (bf16[2,160,640]{2,0,1:T(2,128)(2,1)S(1)}, bf16[2,160,640]{2,0,1:T(2,128)(2,1)S(1)}, u32[]{:S(2)}, u32[]{:S(2)}) collective-permute-start(bf16[2,160,640]{2,0,1:T(2,128)(2,1)S(1)} %collective-permute-done.5), channel_id=1, source_target_pairs={{0,14},{2,0},{4,2},{6,4},{8,6},{10,8},{12,10},{14,12},{1,15},{3,1}... | collective-permute-start | bytes 1228808 | tf_op jit(solution)/shard_map/ppermute | solution.py:12
  59.3 7.4 %copy-start = (bf16[2,8,160,640]{3,2,1,0:T(8,128)(2,1)}, bf16[2,8,160,640]{3,2,1,0:T(8,128)(2,1)S(1)}, u32[]{:S(2)}) copy-start(bf16[2,8,160,640]{3,2,1,0:T(8,128)(2,1)S(1)} %copy_dynamic-update-slice_fusion.10) | copy-start | bytes 9830404
  64.8 17.5 %collective-permute-start.8 = (bf16[2,160,640]{2,0,1:T(2,128)(2,1)S(1)}, bf16[2,160,640]{2,0,1:T(2,128)(2,1)S(1)}, u32[]{:S(2)}, u32[]{:S(2)}) collective-permute-start(bf16[2,160,640]{2,0,1:T(2,128)(2,1)S(1)} %collective-permute-done.6), channel_id=1, source_target_pairs={{0,2},{2,4},{4,6},{6,8},{8,10},{10,12},{12,14},{14,0},{1,3},{3,5},... | collective-permute-start | bytes 1228808 | tf_op jit(solution)/shard_map/ppermute | solution.py:12
  66.7 11.7 %collective-permute-start.9 = (bf16[2,160,640]{2,0,1:T(2,128)(2,1)S(1)}, bf16[2,160,640]{2,0,1:T(2,128)(2,1)S(1)}, u32[]{:S(2)}, u32[]{:S(2)}) collective-permute-start(bf16[2,160,640]{2,0,1:T(2,128)(2,1)S(1)} %collective-permute-done.7), channel_id=1, source_target_pairs={{0,14},{2,0},{4,2},{6,4},{8,6},{10,8},{12,10},{14,12},{1,15},{3,1}... | collective-permute-start | bytes 1228808 | tf_op jit(solution)/shard_map/ppermute | solution.py:12
  71.5 25.3 %collective-permute-start.11 = (bf16[2,8,40,896]{3,1,2,0:T(8,128)(2,1)S(1)}, bf16[2,8,40,896]{3,1,2,0:T(8,128)(2,1)S(1)}, u32[]{:S(2)}, u32[]{:S(2)}) collective-permute-start(bf16[2,8,40,896]{3,1,2,0:T(8,128)(2,1)S(1)} %bitcast.83), channel_id=1, source_target_pairs={{0,16},{16,32},{32,48},{48,0},{1,17},{17,33},{33,49},{49,1},{2,18}... | collective-permute-start | bytes 3440648 | tf_op jit(solution)/shard_map/ppermute | solution.py:12
  74.3 26.4 %collective-permute-start.12 = (bf16[2,8,40,896]{3,1,2,0:T(8,128)(2,1)S(1)}, bf16[2,8,40,896]{3,1,2,0:T(8,128)(2,1)S(1)}, u32[]{:S(2)}, u32[]{:S(2)}) collective-permute-start(bf16[2,8,40,896]{3,1,2,0:T(8,128)(2,1)S(1)} %bitcast.84), channel_id=1, source_target_pairs={{0,48},{16,0},{32,16},{48,32},{1,49},{17,1},{33,17},{49,33},{2,50}... | collective-permute-start | bytes 3440648 | tf_op jit(solution)/shard_map/ppermute | solution.py:12
  78.4 9.0 %collective-permute-start.10 = (bf16[2,160,640]{2,0,1:T(2,128)(2,1)S(1)}, bf16[2,160,640]{2,0,1:T(2,128)(2,1)S(1)}, u32[]{:S(2)}, u32[]{:S(2)}) collective-permute-start(bf16[2,160,640]{2,0,1:T(2,128)(2,1)S(1)} %collective-permute-done.9), channel_id=1, source_target_pairs={{0,14},{2,0},{4,2},{6,4},{8,6},{10,8},{12,10},{14,12},{1,15},{3,1}... | collective-permute-start | bytes 1228808 | tf_op jit(solution)/shard_map/ppermute | solution.py:12
  96.9 12.1 %collective-permute-start.13 = (bf16[2,4,40,896]{3,1,2,0:T(4,128)(2,1)S(1)}, bf16[2,4,40,896]{3,1,2,0:T(4,128)(2,1)S(1)}, u32[]{:S(2)}, u32[]{:S(2)}) collective-permute-start(bf16[2,4,40,896]{3,1,2,0:T(4,128)(2,1)S(1)} %slice.16), channel_id=1, source_target_pairs={{0,16},{16,32},{32,48},{48,0},{1,17},{17,33},{33,49},{49,1},{2,18}... | collective-permute-start | bytes 1720328 | tf_op jit(solution)/shard_map/ppermute | solution.py:12
  101.0 13.0 %collective-permute-start.14 = (bf16[2,4,40,896]{3,1,2,0:T(4,128)(2,1)S(1)}, bf16[2,4,40,896]{3,1,2,0:T(4,128)(2,1)S(1)}, u32[]{:S(2)}, u32[]{:S(2)}) collective-permute-start(bf16[2,4,40,896]{3,1,2,0:T(4,128)(2,1)S(1)} %slice.17), channel_id=1, source_target_pairs={{0,48},{16,0},{32,16},{48,32},{1,49},{17,1},{33,17},{49,33},{2,50}... | collective-permute-start | bytes 1720328 | tf_op jit(solution)/shard_map/ppermute | solution.py:12
  103.4 10.7 %copy-start.1 = (bf16[2,8,160,640]{3,2,1,0:T(8,128)(2,1)S(1)}, bf16[2,8,160,640]{3,2,1,0:T(8,128)(2,1)}, u32[]{:S(2)}) copy-start(bf16[2,8,160,640]{3,2,1,0:T(8,128)(2,1)} %copy_dynamic-update-slice_fusion.5) | copy-start | bytes 9830404
  118.5 1.3 copy-start.2
  121.2 10.0 %collective-permute-start.15 = (bf16[2,4,80,896]{3,2,0,1:T(8,128)(2,1)}, bf16[2,4,80,896]{3,2,0,1:T(8,128)(2,1)S(1)}, u32[]{:S(2)}, u32[]{:S(2)}) collective-permute-start(bf16[2,4,80,896]{3,2,0,1:T(8,128)(2,1)} %fusion.4), channel_id=1, source_target_pairs={{0,64},{64,0},{1,65},{65,1},{2,66},{66,2},{3,67},{67,3},{4,68},{68... | collective-permute-start | bytes 3440648 | tf_op jit(solution)/shard_map/ppermute | solution.py:12
  184.0 6.8 %collective-permute-start.16 = (bf16[320,896]{1,0:T(8,128)(2,1)S(1)}, bf16[320,896]{1,0:T(8,128)(2,1)S(1)}, u32[]{:S(2)}, u32[]{:S(2)}) collective-permute-start(bf16[320,896]{1,0:T(8,128)(2,1)S(1)} %bitcast.77), channel_id=1, source_target_pairs={{0,64},{64,0},{1,65},{65,1},{2,66},{66,2},{3,67},{67,3},{4,68},{68... | collective-permute-start | bytes 1720328 | tf_op jit(solution)/shard_map/ppermute | solution.py:12

commit v2 on v1

v2 whole, which is shorter than its diff:
```python
import functools

import jax
import jax.numpy as jnp
from jax import lax
from jax.experimental import pallas as pl
from jax.experimental.layout import Layout, with_layout_constraint
from jax.experimental.pallas import tpu as pltpu
from jax.sharding import Mesh, PartitionSpec as P

damping = 0.001
axes = ("yhi", "core", "x", "z", "ylo")
far = (2, 1, 3)
back = (1, 3, 2)


def shift(value, axis, by):
    count = lax.axis_size(axis)
    return lax.ppermute(value, axis, [(i, (i + by) % count) for i in range(count)])


def exchange(value, axis):
    return lax.all_to_all(value, axis, split_axis=0, concat_axis=0, tiled=True)


def put(whole, piece, dim, index, split=None, start=0):
    at = [0] * whole.ndim
    at[dim] = index % whole.shape[dim]
    if split is not None:
        at[split] = start
    return lax.dynamic_update_slice(whole, jnp.expand_dims(piece, dim), at)


def plain(value):
    return with_layout_constraint(value, Layout(major_to_minor=tuple(range(value.ndim))))


def room(own, axis, dim):
    shape = list(own.shape)
    shape.insert(dim, lax.axis_size(axis))
    return jnp.zeros(shape, own.dtype)


def product(feats, cots, m):
    lhs = feats[m].reshape(-1, feats.shape[-1])
    rhs = cots[m].reshape(-1, cots.shape[-1])
    return lax.dot_general(lhs, rhs, (((0,), (0,)), ((), ())), preferred_element_type=jnp.float32)


def run(copies, sems):
    made = [pltpu.make_async_copy(source, target, sems.at[i]) for i, (source, target) in enumerate(copies)]
    for copy in made:
        copy.start()
    return made


def early_kernel(count, where, *refs):
    feat_refs, cot_refs, (out, feats, cots, sems) = refs[:count], refs[count:-4], refs[-4:]
    near = len(cot_refs)
    copies = [(ref.at[:, :near], feats.at[:, :, where[i]]) for i, ref in enumerate(feat_refs)]
    copies += [(ref, cots.at[:, i]) for i, ref in enumerate(cot_refs)]
    made = run(copies, sems)
    missing = jnp.zeros(feats.shape[3:], feats.dtype)
    for m in range(out.shape[0]):
        for i in range(near):
            feats[m, i, where[count]] = missing
    for copy in made:
        copy.wait()
    for m in range(out.shape[0]):
        out[m] = product(feats, cots, m)


def late_kernel(count, where, *refs):
    feat_refs, (*near_refs, low, high, partial, weight) = refs[:count], refs[count:-8]
    mine, theirs, feats, cots, held, scale, sems, more = refs[-8:]
    batches, rows = held.shape[:2]
    half, near, zs = low.shape[1], len(near_refs), 2 * low.shape[1]
    copies = [(low, cots.at[:, :half]), (high, cots.at[:, half:zs])]
    copies += [(ref.at[:, near], feats.at[:, where[i]]) for i, ref in enumerate(feat_refs)]
    copies += [(feat_refs[-1].at[:, :near], feats.at[:, zs:])]
    copies += [(ref.at[:, where[count - 1]], cots.at[:, zs + i]) for i, ref in enumerate(near_refs)]
    first = run(copies, sems)
    second = run([(partial, held), (weight, scale)], more)
    for copy in first:
        copy.wait()
    grads = [product(feats, cots, m) for m in range(batches)]
    for copy in second:
        copy.wait()
    for side in range(2):
        part = slice(side * rows // 2, (side + 1) * rows // 2)
        total = 0.0
        for m in range(batches):
            grad = held[m, part, :] + grads[m][part]
            total = total + grad * grad
        term = total / batches + damping
        numer = (term * scale[part, :].astype(jnp.float32)).astype(jnp.bfloat16)
        denom = term.astype(jnp.bfloat16)

        @pl.when(where[count] == side)
        def _(numer=numer, denom=denom):
            mine[0], mine[1] = numer, denom

        @pl.when(where[count] != side)
        def _(numer=numer, denom=denom):
            theirs[0], theirs[1] = numer, denom


def call(kernel, where, feats, others, out, scratch, flops):
    hbm, vmem = pl.BlockSpec(memory_space=pl.ANY), pl.BlockSpec(memory_space=pltpu.VMEM)
    return pl.pallas_call(
        functools.partial(kernel, len(feats)),
        out_shape=out,
        in_specs=[pl.BlockSpec(memory_space=pltpu.SMEM)] + [hbm] * (len(feats) + len(others)),
        out_specs=jax.tree.map(lambda _: vmem, out),
        scratch_shapes=scratch,
        cost_estimate=pl.CostEstimate(flops=flops, bytes_accessed=12 << 20, transcendentals=0),
        compiler_params=pltpu.CompilerParams(vmem_limit_bytes=56 << 20),
    )(where, *feats, *others)


def early_call(where, feats, cots):
    batches, zs, used, cols = cots[0].shape
    rows, near = feats[0].shape[3], len(cots)
    out = jax.ShapeDtypeStruct((batches, rows, cols), jnp.float32)
    scratch = [
        pltpu.VMEM((batches, near, zs, used, rows), jnp.bfloat16),
        pltpu.VMEM((batches, near, zs, used, cols), jnp.bfloat16),
        pltpu.SemaphoreType.DMA((len(feats) + near,)),
    ]
    return call(early_kernel, where, feats, cots, out, scratch, 2 * batches * near * zs * used * rows * cols)


def late_call(where, feats, cots, low, high, partial, weight):
    batches, zs, used, cols = cots[0].shape
    rows, near = feats[0].shape[3], len(cots)
    out = jax.ShapeDtypeStruct((2, rows // 2, cols), jnp.bfloat16)
    scratch = [
        pltpu.VMEM((batches, zs + near, used, rows), jnp.bfloat16),
        pltpu.VMEM((batches, zs + near, used, cols), jnp.bfloat16),
        pltpu.VMEM((batches, rows, cols), jnp.float32),
        pltpu.VMEM((rows, cols), jnp.bfloat16),
        pltpu.SemaphoreType.DMA((len(feats) + near + 3,)),
        pltpu.SemaphoreType.DMA((2,)),
    ]
    others = [*cots, low, high, partial, weight]
    flops = 2 * batches * (zs + near) * used * rows * cols
    return call(late_kernel, where, feats, others, (out, out), scratch, flops)


def body(weights, activations, cotangents, lengths):
    xs, zs, ys = (lax.axis_size(a) for a in ("x", "z", "ylo"))
    cores, his = lax.axis_size("core"), lax.axis_size("yhi")
    x, z, y, core = (lax.axis_index(a) for a in ("x", "z", "ylo", "core"))
    rows, cols = weights.shape[2:]
    batches, slots = activations.shape[1:3]

    cots = cotangents[0].transpose(1, 0, 2).reshape(slots, batches, zs * ys, cols).transpose(2, 0, 1, 3)
    cots = exchange(cots, ("z", "ylo"))
    cots = cots.transpose(2, 0, 1, 3).reshape(batches, zs, ys * slots, cols)

    mask = (jnp.arange(slots)[None, :] < lengths[0, :, 0:1]).astype(jnp.bfloat16)
    feats = activations[0] * mask[:, :, None]
    feats = feats.transpose(1, 0, 2).reshape(slots, batches, xs, rows).transpose(2, 0, 1, 3)
    blocks = [lax.dynamic_index_in_dim(feats, (x + k) % xs, 0, keepdims=False) for k in range(xs)]
    plane = plain(jnp.stack([blocks[0]] + [shift(blocks[k], "x", k) for k in back]))
    pair = put(room(plane, "ylo", 1), plane, 1, y)
    pair = plain(put(pair, shift(plane, "ylo", 1), 1, 1 - y))
    own = pair.transpose(3, 0, 1, 2, 4).reshape(batches, xs, ys * slots, rows)

    up = down = own
    pieces, places = [own], [0]
    for k in range(1, zs // 2):
        up, down = shift(up, "z", 1), shift(down, "z", -1)
        pieces, places = pieces + [up, down], places + [-k, k]
    pieces, places = pieces + [shift(down, "z", -1)], places + [zs // 2]

    half = zs // 2
    left, right = shift(cots, "x", 1), shift(cots, "x", -1)
    first, second = shift(left[:, :half], "x", 1), shift(right[:, half:], "x", -1)

    zat = [(z + at) % zs for at in places]
    near = [cots, left, right]
    partial = early_call(jnp.stack(zat).astype(jnp.int32), pieces[:-1], near)
    where = jnp.stack(zat + [core]).astype(jnp.int32)
    mine, theirs = late_call(where, pieces, near, first, second, partial, weights[0, 0])
    other = shift(theirs, "core", 1)
    both = (mine.astype(jnp.float32) + other.astype(jnp.float32)).astype(jnp.bfloat16)
    both = both.reshape(2, his, rows // cores // his, cols).transpose(1, 0, 2, 3)
    high = lax.axis_index("yhi")
    sums = lax.dynamic_index_in_dim(both, high, 0, keepdims=False).astype(jnp.float32)
    parts = [lax.dynamic_index_in_dim(both, (high + k) % his, 0, keepdims=False) for k in far]
    for k, part in zip(far, parts):
        sums = sums + shift(part, "yhi", k).astype(jnp.float32)
    merged = (sums[0] / sums[1]).astype(jnp.bfloat16)
    merged = exchange(jnp.broadcast_to(merged[None], (his,) + merged.shape), "yhi")
    merged = merged.reshape(rows // cores, cols)
    other = shift(merged, "core", 1)
    out = jnp.where(core == 0, jnp.stack([merged, other]), jnp.stack([other, merged]))
    return out.reshape(1, rows, cols)


def solution(mesh):
    inner = Mesh(mesh.devices.reshape(4, 2, 4, 8, 2), axes)
    dom, fsdp = axes[:2], axes[2:]
    return jax.shard_map(
        body,
        mesh=inner,
        in_specs=(
            P(dom, fsdp, None, None),
            P(dom, None, fsdp, None),
            P(dom, None, fsdp, None),
            P(dom, None, fsdp),
        ),
        out_specs=P(fsdp, None, None),
        check_vma=False,
    )
```

time: 193 us -> 185 us (0.959)
  the two profiles are of different devices: /device:TPU:15 before, /device:TPU:1 now
where the time goes in v2:
time: 185 us; the launch traced here: 184 us
  starting transfers between devices  90.6 us (49%)
  waiting for transfers between devices  42.5 us (23%)
  blocking collectives  17.9 us (10%)
  Pallas kernels  16.9 us (9%)
  local copies, waits for them, and re-layouts  11.1 us (6%)
  other arithmetic  4.18 us (2%)
    ppermute x20, starting transfers between devices, shift(): lax.ppermute(value, axis, [(i, (i + by) % count) for i in range(count)])  78.5 us
    ppermute x20, waiting for transfers between devices, shift(): lax.ppermute(value, axis, [(i, (i + by) % count) for i in range(count)])  33.9 us
    all_to_all x1, blocking collectives, exchange(): return lax.all_to_all(value, axis, split_axis=0, concat_axis=0, tiled=True)  17.9 us
    pallas_call x2, Pallas kernels, call(): pl.pallas_call(functools.partial(kernel, len(feats)), out_shape=out, in_s...  16.9 us
    all_to_all x1, starting transfers between devices, exchange(): return lax.all_to_all(value, axis, split_axis=0, concat_axis=0, tiled=True)  12.1 us
    all_to_all x1, waiting for transfers between devices, exchange(): return lax.all_to_all(value, axis, split_axis=0, concat_axis=0, tiled=True)  8.63 us
  transfers between devices with their start and end apart: 21, of which 9 were waited for; matrix products, arithmetic and copies ran while one was open for 4% of the time, Pallas kernels for 5%

profile of v2, /device:TPU:1, one launch (start us, length us, event | category | flops | bytes accessed | tf_op | source)
XLA Modules:
  0.0 184.0 jit_solution(10639871579274855011)
XLA Ops:
  0.0 3.0 %copy.37 = bf16[20,1,16,2,896]{4,3,1,0,2:T(2,128)(2,1)} copy(bf16[20,1,16,2,896]{4,3,2,1,0:T(2,128)(2,1)} %bitcast.73) | data formatting | bytes 2293760 | tf_op jit(solution)/shard_map/reshape | solution.py:157
  3.1 12.1 %all-to-all-start = ((bf16[16,20,2,896]{3,2,1,0:T(2,128)(2,1)}), bf16[16,20,2,896]{3,2,1,0:T(2,128)(2,1)S(1)}, u32[]{:S(2)}, u32[]{:S(2)}) async-start(bf16[16,20,2,896]{3,2,1,0:T(2,128)(2,1)} %bitcast.63), calls=%async_computation | async-start | bytes 2293760 | tf_op jit(solution)/shard_map/all_to_all | solution.py:23
  15.2 0.3 fusion.3
  15.5 0.1 reshape.80
  15.7 0.4 constant_dynamic-slice_fusion.3
  16.1 0.1 copy.40
  16.2 3.1 %collective-permute-start = (bf16[20,2,640]{2,1,0:T(2,128)(2,1)S(1)}, bf16[20,2,640]{2,1,0:T(2,128)(2,1)S(1)}, u32[]{:S(2)}, u32[]{:S(2)}) collective-permute-start(bf16[20,2,640]{2,1,0:T(2,128)(2,1)S(1)} %bitcast.77), channel_id=1, source_target_pairs={{0,16},{16,32},{32,48},{48,0},{1,17},{17,33},{33,49},{49,1},{2,18}... | collective-permute-start | bytes 153608 | tf_op jit(solution)/shard_map/ppermute | solution.py:19
  19.3 0.1 copy.39
  19.4 3.4 %collective-permute-start.1 = (bf16[20,2,640]{2,1,0:T(2,128)(2,1)S(1)}, bf16[20,2,640]{2,1,0:T(2,128)(2,1)S(1)}, u32[]{:S(2)}, u32[]{:S(2)}) collective-permute-start(bf16[20,2,640]{2,1,0:T(2,128)(2,1)S(1)} %bitcast.78), channel_id=1, source_target_pairs={{0,48},{16,0},{32,16},{48,32},{1,49},{17,1},{33,17},{49,33},{2,50}... | collective-permute-start | bytes 153608 | tf_op jit(solution)/shard_map/ppermute | solution.py:19
  22.7 0.1 copy.38
  22.8 3.4 %collective-permute-start.2 = (bf16[20,2,640]{2,1,0:T(2,128)(2,1)S(1)}, bf16[20,2,640]{2,1,0:T(2,128)(2,1)S(1)}, u32[]{:S(2)}, u32[]{:S(2)}) collective-permute-start(bf16[20,2,640]{2,1,0:T(2,128)(2,1)S(1)} %bitcast.79), channel_id=1, source_target_pairs={{0,32},{16,48},{32,0},{48,16},{1,33},{17,49},{33,1},{49,17},{2,34}... | collective-permute-start | bytes 153608 | tf_op jit(solution)/shard_map/ppermute | solution.py:19
  26.3 0.1 copy.41
  26.3 0.0 collective-permute-done
  26.4 3.1 %collective-permute-done.2 = bf16[20,2,640]{2,1,0:T(2,128)(2,1)S(1)} collective-permute-done((bf16[20,2,640]{2,1,0:T(2,128)(2,1)S(1)}, bf16[20,2,640]{2,1,0:T(2,128)(2,1)S(1)}, u32[]{:S(2)}, u32[]{:S(2)}) %collective-permute-start.2) | collective-permute-done | bytes 51232 | tf_op jit(solution)/shard_map/ppermute | solution.py:19
  29.5 1.0 broadcast_in_dim.19
  30.4 1.0 bitcast_dynamic-update-slice_fusion.1
  31.4 3.1 %collective-permute-start.3 = (bf16[4,20,2,640]{3,2,1,0:T(2,128)(2,1)}, bf16[4,20,2,640]{3,2,1,0:T(2,128)(2,1)}, u32[]{:S(2)}, u32[]{:S(2)}) collective-permute-start(bf16[4,20,2,640]{3,2,1,0:T(2,128)(2,1)} %get-tuple-element.10), channel_id=1, source_target_pairs={{0,1},{1,0},{2,3},{3,2},{4,5},{5,4},{6,7},{7,6},{8,9},{9,8},{10,11... | collective-permute-start | bytes 614408 | tf_op jit(solution)/shard_map/ppermute | solution.py:19
  34.5 8.6 %all-to-all-done = bf16[16,20,2,896]{3,2,1,0:T(2,128)(2,1)S(1)} async-done(((bf16[16,20,2,896]{3,2,1,0:T(2,128)(2,1)}), bf16[16,20,2,896]{3,2,1,0:T(2,128)(2,1)S(1)}, u32[]{:S(2)}, u32[]{:S(2)}) %all-to-all-start) | async-done | bytes 1146912 | tf_op jit(solution)/shard_map/all_to_all | solution.py:23
  43.1 0.1 copy.24.refs_7_.refs_8_
  43.3 0.0 copy-start
  43.3 3.1 %collective-permute-start.11 = (bf16[2,8,40,896]{3,2,1,0:T(8,128)(2,1)S(1)}, bf16[2,8,40,896]{3,2,1,0:T(8,128)(2,1)S(1)}, u32[]{:S(2)}, u32[]{:S(2)}) collective-permute-start(bf16[2,8,40,896]{3,2,1,0:T(8,128)(2,1)S(1)} %copy.24.refs_7_.refs_8_), channel_id=1, source_target_pairs={{0,16},{16,32},{32,48},{48,0},{1,17},{17,33},{33,49},{49,1},{2,18}... | collective-permute-start | bytes 3440648 | tf_op jit(solution)/shard_map/ppermute | solution.py:19
  46.4 3.4 %collective-permute-start.12 = (bf16[2,8,40,896]{3,2,1,0:T(8,128)(2,1)S(1)}, bf16[2,8,40,896]{3,2,1,0:T(8,128)(2,1)S(1)}, u32[]{:S(2)}, u32[]{:S(2)}) collective-permute-start(bf16[2,8,40,896]{3,2,1,0:T(8,128)(2,1)S(1)} %copy.24.refs_7_.refs_8_), channel_id=1, source_target_pairs={{0,48},{16,0},{32,16},{48,32},{1,49},{17,1},{33,17},{49,33},{2,50}... | collective-permute-start | bytes 3440648 | tf_op jit(solution)/shard_map/ppermute | solution.py:19
  49.8 0.0 collective-permute-done.3
  49.8 1.8 bitcast_dynamic-update-slice_fusion
  51.6 1.0 copy.23.refs_0_
  52.6 2.6 %collective-permute-start.5 = (bf16[2,4,40,640]{3,2,1,0:T(8,128)(2,1)S(1)}, bf16[2,4,40,640]{3,2,1,0:T(8,128)(2,1)S(1)}, u32[]{:S(2)}, u32[]{:S(2)}) collective-permute-start(bf16[2,4,40,640]{3,2,1,0:T(8,128)(2,1)S(1)} %copy.23.refs_0_), channel_id=1, source_target_pairs={{0,14},{2,0},{4,2},{6,4},{8,6},{10,8},{12,10},{14,12},{1,15},{3,1}... | collective-permute-start | bytes 1228808 | tf_op jit(solution)/shard_map/ppermute | solution.py:19
  55.2 2.7 %collective-permute-start.4 = (bf16[2,4,40,640]{3,2,1,0:T(8,128)(2,1)S(1)}, bf16[2,4,40,640]{3,2,1,0:T(8,128)(2,1)S(1)}, u32[]{:S(2)}, u32[]{:S(2)}) collective-permute-start(bf16[2,4,40,640]{3,2,1,0:T(8,128)(2,1)S(1)} %copy.23.refs_0_), channel_id=1, source_target_pairs={{0,2},{2,4},{4,6},{6,8},{8,10},{10,12},{12,14},{14,0},{1,3},{3,5},... | collective-permute-start | bytes 1228808 | tf_op jit(solution)/shard_map/ppermute | solution.py:19
  57.9 4.3 %collective-permute-done.5.refs_2_ = bf16[2,4,40,640]{3,2,1,0:T(8,128)(2,1)S(1)} collective-permute-done((bf16[2,4,40,640]{3,2,1,0:T(8,128)(2,1)S(1)}, bf16[2,4,40,640]{3,2,1,0:T(8,128)(2,1)S(1)}, u32[]{:S(2)}, u32[]{:S(2)}) %collective-permute-start.5) | collective-permute-done | bytes 409632 | tf_op jit(solution)/shard_map/ppermute | solution.py:19
  62.3 4.4 %collective-permute-start.7 = (bf16[2,4,40,640]{3,2,1,0:T(8,128)(2,1)S(1)}, bf16[2,4,40,640]{3,2,1,0:T(8,128)(2,1)S(1)}, u32[]{:S(2)}, u32[]{:S(2)}) collective-permute-start(bf16[2,4,40,640]{3,2,1,0:T(8,128)(2,1)S(1)} %collective-permute-done.5.refs_2_), channel_id=1, source_target_pairs={{0,14},{2,0},{4,2},{6,4},{8,6},{10,8},{12,10},{14,12},{1,15},{3,1}... | collective-permute-start | bytes 1228808 | tf_op jit(solution)/shard_map/ppermute | solution.py:19
  66.7 0.0 collective-permute-done.4.refs_1_
  66.7 1.9 %collective-permute-start.6 = (bf16[2,4,40,640]{3,2,1,0:T(8,128)(2,1)S(1)}, bf16[2,4,40,640]{3,2,1,0:T(8,128)(2,1)}, u32[]{:S(2)}, u32[]{:S(2)}) collective-permute-start(bf16[2,4,40,640]{3,2,1,0:T(8,128)(2,1)S(1)} %collective-permute-done.4.refs_1_), channel_id=1, source_target_pairs={{0,2},{2,4},{4,6},{6,8},{8,10},{10,12},{12,14},{14,0},{1,3},{3,5},... | collective-permute-start | bytes 1228808 | tf_op jit(solution)/shard_map/ppermute | solution.py:19
  68.6 3.3 %collective-permute-done.7.refs_4_ = bf16[2,4,40,640]{3,2,1,0:T(8,128)(2,1)S(1)} collective-permute-done((bf16[2,4,40,640]{3,2,1,0:T(8,128)(2,1)S(1)}, bf16[2,4,40,640]{3,2,1,0:T(8,128)(2,1)S(1)}, u32[]{:S(2)}, u32[]{:S(2)}) %collective-permute-start.7) | collective-permute-done | bytes 409632 | tf_op jit(solution)/shard_map/ppermute | solution.py:19
  72.0 5.3 %collective-permute-start.9 = (bf16[2,4,40,640]{3,2,1,0:T(8,128)(2,1)S(1)}, bf16[2,4,40,640]{3,2,1,0:T(8,128)(2,1)}, u32[]{:S(2)}, u32[]{:S(2)}) collective-permute-start(bf16[2,4,40,640]{3,2,1,0:T(8,128)(2,1)S(1)} %collective-permute-done.7.refs_4_), channel_id=1, source_target_pairs={{0,14},{2,0},{4,2},{6,4},{8,6},{10,8},{12,10},{14,12},{1,15},{3,1}... | collective-permute-start | bytes 1228808 | tf_op jit(solution)/shard_map/ppermute | solution.py:19
  77.3 2.9 %collective-permute-start.8 = (bf16[2,4,40,640]{3,2,1,0:T(8,128)(2,1)}, bf16[2,4,40,640]{3,2,1,0:T(8,128)(2,1)}, u32[]{:S(2)}, u32[]{:S(2)}) collective-permute-start(bf16[2,4,40,640]{3,2,1,0:T(8,128)(2,1)} %collective-permute-done.6.refs_3_), channel_id=1, source_target_pairs={{0,2},{2,4},{4,6},{6,8},{8,10},{10,12},{12,14},{14,0},{1,3},{3,5},... | collective-permute-start | bytes 1228808 | tf_op jit(solution)/shard_map/ppermute | solution.py:19
  80.3 0.9 slice.16
  81.2 1.9 %collective-permute-start.13 = (bf16[2,4,40,896]{3,2,1,0:T(8,128)(2,1)}, bf16[2,4,40,896]{3,2,1,0:T(8,128)(2,1)}, u32[]{:S(2)}, u32[]{:S(2)}) collective-permute-start(bf16[2,4,40,896]{3,2,1,0:T(8,128)(2,1)} %slice.16), channel_id=1, source_target_pairs={{0,16},{16,32},{32,48},{48,0},{1,17},{17,33},{33,49},{49,1},{2,18}... | collective-permute-start | bytes 1720328 | tf_op jit(solution)/shard_map/ppermute | solution.py:19
  83.1 0.0 collective-permute-done.12.refs_9_.refs_10_
  83.2 4.6 %collective-permute-start.14 = (bf16[2,4,40,896]{3,2,1,0:T(8,128)(2,1)S(1)}, bf16[2,4,40,896]{3,2,1,0:T(8,128)(2,1)S(1)}, u32[]{:S(2)}, u32[]{:S(2)}) collective-permute-start(bf16[2,4,40,896]{3,2,1,0:T(8,128)(2,1)S(1)} %slice.17), channel_id=1, source_target_pairs={{0,48},{16,0},{32,16},{48,32},{1,49},{17,1},{33,17},{49,33},{2,50}... | collective-permute-start | bytes 1720328 | tf_op jit(solution)/shard_map/ppermute | solution.py:19
  87.8 0.0 collective-permute-done.9.refs_6_
  87.8 3.6 %collective-permute-start.10 = (bf16[2,4,40,640]{3,2,1,0:T(8,128)(2,1)}, bf16[2,4,40,640]{3,2,1,0:T(8,128)(2,1)S(1)}, u32[]{:S(2)}, u32[]{:S(2)}) collective-permute-start(bf16[2,4,40,640]{3,2,1,0:T(8,128)(2,1)} %collective-permute-done.9.refs_6_), channel_id=1, source_target_pairs={{0,14},{2,0},{4,2},{6,4},{8,6},{10,8},{12,10},{14,12},{1,15},{3,1}... | collective-permute-start | bytes 1228808 | tf_op jit(solution)/shard_map/ppermute | solution.py:19
  91.5 0.7 stack.78.where
  92.2 0.6 stack.73.where
  92.8 0.0 collective-permute-done.8.refs_5_
  92.8 8.4 %shard_map.46.refs_13_ = f32[2,640,896]{2,1,0:T(8,128)} custom-call(s32[8]{0:T(128)} %stack.78.where, bf16[2,4,40,640]{3,2,1,0:T(8,128)(2,1)} %copy-done.3, bf16[2,4,40,640]{3,2,1,0:T(8,128)(2,1)} %copy-done.5, bf16[2,4,40,640]{3,2,1,0:T(8,128)(2,1)} %copy-done.4, bf16[2,4,40,640]{3,2,1,0:T(8,128)(2,1)} %collective-permute-done.6.refs_3_, ...), custom_call_target="tpu_custom_call" | custom-call | flops 2202009600 | bytes 12582912 | tf_op jit(solution)/shard_map/pallas_call | solution.py:110
  101.2 0.0 collective-permute-done.10.refs_7_
  101.2 0.0 collective-permute-done.14.refs_12_
  101.2 0.7 copy-done.8
  102.0 0.2 copy-done.7
  102.2 8.5 %shard_map.47 = (bf16[2,320,896]{2,1,0:T(8,128)(2,1)}, bf16[2,320,896]{2,1,0:T(8,128)(2,1)}) custom-call(s32[9]{0:T(128)} %stack.73.where, bf16[2,4,40,640]{3,2,1,0:T(8,128)(2,1)} %copy-done.3, bf16[2,4,40,640]{3,2,1,0:T(8,128)(2,1)} %copy-done.5, bf16[2,4,40,640]{3,2,1,0:T(8,128)(2,1)} %copy-done.4, bf16[2,4,40,640]{3,2,1,0:T(8,128)(2,1)} %collective-permute-done.6.refs_3_, ...), custom_call_target="tpu_custom_call" | custom-call | flops 1009254400 | bytes 12582912 | tf_op jit(solution)/shard_map/pallas_call | solution.py:110
  110.7 7.7 %collective-permute-start.15 = (bf16[2,320,896]{2,1,0:T(8,128)(2,1)}, bf16[2,320,896]{2,1,0:T(8,128)(2,1)S(1)}, u32[]{:S(2)}, u32[]{:S(2)}) collective-permute-start(bf16[2,320,896]{2,1,0:T(8,128)(2,1)} %get-tuple-element.8), channel_id=1, source_target_pairs={{0,64},{64,0},{1,65},{65,1},{2,66},{66,2},{3,67},{67,3},{4,68},{68... | collective-permute-start | bytes 3440648 | tf_op jit(solution)/shard_map/ppermute | solution.py:19
  118.4 2.6 %collective-permute-done.15 = bf16[2,320,896]{2,1,0:T(8,128)(2,1)S(1)} collective-permute-done((bf16[2,320,896]{2,1,0:T(8,128)(2,1)}, bf16[2,320,896]{2,1,0:T(8,128)(2,1)S(1)}, u32[]{:S(2)}, u32[]{:S(2)}) %collective-permute-start.15) | collective-permute-done | bytes 1146912 | tf_op jit(solution)/shard_map/ppermute | solution.py:19
  121.0 1.5 add_convert_fusion
  122.5 0.1 dynamic-slice_bitcast_fusion.2
  122.6 6.6 %collective-permute-start.16 = (bf16[2,80,896]{2,1,0:T(8,128)(2,1)S(1)}, bf16[2,80,896]{2,1,0:T(8,128)(2,1)S(1)}, u32[]{:S(2)}, u32[]{:S(2)}) collective-permute-start(bf16[2,80,896]{2,1,0:T(8,128)(2,1)S(1)} %get-tuple-element.11), channel_id=1, source_target_pairs={{0,256},{128,384},{256,0},{384,128},{1,257},{129,385},{257,1},{385... | collective-permute-start | bytes 860168 | tf_op jit(solution)/shard_map/ppermute | solution.py:19
  129.2 2.4 %collective-permute-start.17 = (bf16[2,80,896]{2,1,0:T(8,128)(2,1)S(1)}, bf16[2,80,896]{2,1,0:T(8,128)(2,1)S(1)}, u32[]{:S(2)}, u32[]{:S(2)}) collective-permute-start(bf16[2,80,896]{2,1,0:T(8,128)(2,1)S(1)} %get-tuple-element.13), channel_id=1, source_target_pairs={{0,128},{128,256},{256,384},{384,0},{1,129},{129,257},{257,385},{3... | collective-permute-start | bytes 860168 | tf_op jit(solution)/shard_map/ppermute | solution.py:19
  131.6 5.0 %collective-permute-start.18 = (bf16[2,80,896]{2,1,0:T(8,128)(2,1)S(1)}, bf16[2,80,896]{2,1,0:T(8,128)(2,1)S(1)}, u32[]{:S(2)}, u32[]{:S(2)}) collective-permute-start(bf16[2,80,896]{2,1,0:T(8,128)(2,1)S(1)} %get-tuple-element.12), channel_id=1, source_target_pairs={{0,384},{128,0},{256,128},{384,256},{1,385},{129,1},{257,129},{385... | collective-permute-start | bytes 860168 | tf_op jit(solution)/shard_map/ppermute | solution.py:19
  136.6 1.6 collective-permute-done.16
  138.2 11.4 %collective-permute-done.17 = bf16[2,80,896]{2,1,0:T(8,128)(2,1)S(1)} collective-permute-done((bf16[2,80,896]{2,1,0:T(8,128)(2,1)S(1)}, bf16[2,80,896]{2,1,0:T(8,128)(2,1)S(1)}, u32[]{:S(2)}, u32[]{:S(2)}) %collective-permute-start.17) | collective-permute-done | bytes 286752 | tf_op jit(solution)/shard_map/ppermute | solution.py:19
  149.6 5.9 %collective-permute-done.18 = bf16[2,80,896]{2,1,0:T(8,128)(2,1)S(1)} collective-permute-done((bf16[2,80,896]{2,1,0:T(8,128)(2,1)S(1)}, bf16[2,80,896]{2,1,0:T(8,128)(2,1)S(1)}, u32[]{:S(2)}, u32[]{:S(2)}) %collective-permute-start.18) | collective-permute-done | bytes 286752 | tf_op jit(solution)/shard_map/ppermute | solution.py:19
  155.5 0.1 fusion.1
  155.8 17.9 %all_to_all.10 = bf16[4,80,896]{2,1,0:T(8,128)(2,1)S(1)} all-to-all(bf16[4,80,896]{2,1,0:T(8,128)(2,1)S(1)} %broadcast_in_dim.23), channel_id=1, replica_groups=mesh['yhi'=4,'core'=2,'x'=4,'z'=8,'ylo'=2] {'yhi'}, dimensions={0} | all-to-all | bytes 1146880 | tf_op jit(solution)/shard_map/all_to_all | solution.py:23
  173.7 7.5 %collective-permute-start.19 = (bf16[320,896]{1,0:T(8,128)(2,1)S(1)}, bf16[320,896]{1,0:T(8,128)(2,1)S(1)}, u32[]{:S(2)}, u32[]{:S(2)}) collective-permute-start(bf16[320,896]{1,0:T(8,128)(2,1)S(1)} %bitcast.71), channel_id=1, source_target_pairs={{0,64},{64,0},{1,65},{65,1},{2,66},{66,2},{3,67},{67,3},{4,68},{68... | collective-permute-start | bytes 1720328 | tf_op jit(solution)/shard_map/ppermute | solution.py:19
  181.2 1.6 collective-permute-done.19
  182.8 1.2 maximum_select_fusion
  (27 shorter events, 0.2 us)
Async XLA Ops:
  3.0 12.2 %copy-start.10 = (s32[1,2,1]{1,2,0:T(1,128)S(1)}, s32[1,2,1]{1,2,0:T(1,128)}, u32[]{:S(2)}) copy-start(s32[1,2,1]{1,2,0:T(1,128)} %param.7) | copy-start | bytes 28
  3.0 12.2 %copy-start.9 = (bf16[1,2,20,2560]{3,1,2,0:T(2,128)(2,1)S(1)}, bf16[1,2,20,2560]{3,1,2,0:T(2,128)(2,1)}, u32[]{:S(2)}) copy-start(bf16[1,2,20,2560]{3,1,2,0:T(2,128)(2,1)} %param.5) | copy-start | bytes 614404
  3.1 40.1 %all-to-all-start = ((bf16[16,20,2,896]{3,2,1,0:T(2,128)(2,1)}), bf16[16,20,2,896]{3,2,1,0:T(2,128)(2,1)S(1)}, u32[]{:S(2)}, u32[]{:S(2)}) async-start(bf16[16,20,2,896]{3,2,1,0:T(2,128)(2,1)} %bitcast.63), calls=%async_computation | async-start | bytes 2293760 | tf_op jit(solution)/shard_map/all_to_all | solution.py:23
  16.2 10.2 %collective-permute-start = (bf16[20,2,640]{2,1,0:T(2,128)(2,1)S(1)}, bf16[20,2,640]{2,1,0:T(2,128)(2,1)S(1)}, u32[]{:S(2)}, u32[]{:S(2)}) collective-permute-start(bf16[20,2,640]{2,1,0:T(2,128)(2,1)S(1)} %bitcast.77), channel_id=1, source_target_pairs={{0,16},{16,32},{32,48},{48,0},{1,17},{17,33},{33,49},{49,1},{2,18}... | collective-permute-start | bytes 153608 | tf_op jit(solution)/shard_map/ppermute | solution.py:19
  19.4 7.0 %collective-permute-start.1 = (bf16[20,2,640]{2,1,0:T(2,128)(2,1)S(1)}, bf16[20,2,640]{2,1,0:T(2,128)(2,1)S(1)}, u32[]{:S(2)}, u32[]{:S(2)}) collective-permute-start(bf16[20,2,640]{2,1,0:T(2,128)(2,1)S(1)} %bitcast.78), channel_id=1, source_target_pairs={{0,48},{16,0},{32,16},{48,32},{1,49},{17,1},{33,17},{49,33},{2,50}... | collective-permute-start | bytes 153608 | tf_op jit(solution)/shard_map/ppermute | solution.py:19
  22.8 6.7 %collective-permute-start.2 = (bf16[20,2,640]{2,1,0:T(2,128)(2,1)S(1)}, bf16[20,2,640]{2,1,0:T(2,128)(2,1)S(1)}, u32[]{:S(2)}, u32[]{:S(2)}) collective-permute-start(bf16[20,2,640]{2,1,0:T(2,128)(2,1)S(1)} %bitcast.79), channel_id=1, source_target_pairs={{0,32},{16,48},{32,0},{48,16},{1,33},{17,49},{33,1},{49,17},{2,34}... | collective-permute-start | bytes 153608 | tf_op jit(solution)/shard_map/ppermute | solution.py:19
  31.4 18.4 %collective-permute-start.3 = (bf16[4,20,2,640]{3,2,1,0:T(2,128)(2,1)}, bf16[4,20,2,640]{3,2,1,0:T(2,128)(2,1)}, u32[]{:S(2)}, u32[]{:S(2)}) collective-permute-start(bf16[4,20,2,640]{3,2,1,0:T(2,128)(2,1)} %get-tuple-element.10), channel_id=1, source_target_pairs={{0,1},{1,0},{2,3},{3,2},{4,5},{5,4},{6,7},{7,6},{8,9},{9,8},{10,11... | collective-permute-start | bytes 614408 | tf_op jit(solution)/shard_map/ppermute | solution.py:19
  43.3 37.9 %copy-start = (bf16[2,8,40,896]{3,2,1,0:T(8,128)(2,1)}, bf16[2,8,40,896]{3,2,1,0:T(8,128)(2,1)S(1)}, u32[]{:S(2)}) copy-start(bf16[2,8,40,896]{3,2,1,0:T(8,128)(2,1)S(1)} %copy.24.refs_7_.refs_8_) | copy-start | bytes 3440644
  43.3 37.0 %collective-permute-start.11 = (bf16[2,8,40,896]{3,2,1,0:T(8,128)(2,1)S(1)}, bf16[2,8,40,896]{3,2,1,0:T(8,128)(2,1)S(1)}, u32[]{:S(2)}, u32[]{:S(2)}) collective-permute-start(bf16[2,8,40,896]{3,2,1,0:T(8,128)(2,1)S(1)} %copy.24.refs_7_.refs_8_), channel_id=1, source_target_pairs={{0,16},{16,32},{32,48},{48,0},{1,17},{17,33},{33,49},{49,1},{2,18}... | collective-permute-start | bytes 3440648 | tf_op jit(solution)/shard_map/ppermute | solution.py:19
  46.4 36.7 %collective-permute-start.12 = (bf16[2,8,40,896]{3,2,1,0:T(8,128)(2,1)S(1)}, bf16[2,8,40,896]{3,2,1,0:T(8,128)(2,1)S(1)}, u32[]{:S(2)}, u32[]{:S(2)}) collective-permute-start(bf16[2,8,40,896]{3,2,1,0:T(8,128)(2,1)S(1)} %copy.24.refs_7_.refs_8_), channel_id=1, source_target_pairs={{0,48},{16,0},{32,16},{48,32},{1,49},{17,1},{33,17},{49,33},{2,50}... | collective-permute-start | bytes 3440648 | tf_op jit(solution)/shard_map/ppermute | solution.py:19
  52.6 24.7 %copy-start.3 = (bf16[2,4,40,640]{3,2,1,0:T(8,128)(2,1)}, bf16[2,4,40,640]{3,2,1,0:T(8,128)(2,1)S(1)}, u32[]{:S(2)}) copy-start(bf16[2,4,40,640]{3,2,1,0:T(8,128)(2,1)S(1)} %copy.23.refs_0_) | copy-start | bytes 1228804
  52.6 9.6 %collective-permute-start.5 = (bf16[2,4,40,640]{3,2,1,0:T(8,128)(2,1)S(1)}, bf16[2,4,40,640]{3,2,1,0:T(8,128)(2,1)S(1)}, u32[]{:S(2)}, u32[]{:S(2)}) collective-permute-start(bf16[2,4,40,640]{3,2,1,0:T(8,128)(2,1)S(1)} %copy.23.refs_0_), channel_id=1, source_target_pairs={{0,14},{2,0},{4,2},{6,4},{8,6},{10,8},{12,10},{14,12},{1,15},{3,1}... | collective-permute-start | bytes 1228808 | tf_op jit(solution)/shard_map/ppermute | solution.py:19
  55.2 11.5 %collective-permute-start.4 = (bf16[2,4,40,640]{3,2,1,0:T(8,128)(2,1)S(1)}, bf16[2,4,40,640]{3,2,1,0:T(8,128)(2,1)S(1)}, u32[]{:S(2)}, u32[]{:S(2)}) collective-permute-start(bf16[2,4,40,640]{3,2,1,0:T(8,128)(2,1)S(1)} %copy.23.refs_0_), channel_id=1, source_target_pairs={{0,2},{2,4},{4,6},{6,8},{8,10},{10,12},{12,14},{14,0},{1,3},{3,5},... | collective-permute-start | bytes 1228808 | tf_op jit(solution)/shard_map/ppermute | solution.py:19
  62.3 18.0 %copy-start.4 = (bf16[2,4,40,640]{3,2,1,0:T(8,128)(2,1)}, bf16[2,4,40,640]{3,2,1,0:T(8,128)(2,1)S(1)}, u32[]{:S(2)}) copy-start(bf16[2,4,40,640]{3,2,1,0:T(8,128)(2,1)S(1)} %collective-permute-done.5.refs_2_) | copy-start | bytes 1228804
  62.3 9.7 %collective-permute-start.7 = (bf16[2,4,40,640]{3,2,1,0:T(8,128)(2,1)S(1)}, bf16[2,4,40,640]{3,2,1,0:T(8,128)(2,1)S(1)}, u32[]{:S(2)}, u32[]{:S(2)}) collective-permute-start(bf16[2,4,40,640]{3,2,1,0:T(8,128)(2,1)S(1)} %collective-permute-done.5.refs_2_), channel_id=1, source_target_pairs={{0,14},{2,0},{4,2},{6,4},{8,6},{10,8},{12,10},{14,12},{1,15},{3,1}... | collective-permute-start | bytes 1228808 | tf_op jit(solution)/shard_map/ppermute | solution.py:19
  66.7 13.5 %copy-start.5 = (bf16[2,4,40,640]{3,2,1,0:T(8,128)(2,1)}, bf16[2,4,40,640]{3,2,1,0:T(8,128)(2,1)S(1)}, u32[]{:S(2)}) copy-start(bf16[2,4,40,640]{3,2,1,0:T(8,128)(2,1)S(1)} %collective-permute-done.4.refs_1_) | copy-start | bytes 1228804
  66.7 10.6 %collective-permute-start.6 = (bf16[2,4,40,640]{3,2,1,0:T(8,128)(2,1)S(1)}, bf16[2,4,40,640]{3,2,1,0:T(8,128)(2,1)}, u32[]{:S(2)}, u32[]{:S(2)}) collective-permute-start(bf16[2,4,40,640]{3,2,1,0:T(8,128)(2,1)S(1)} %collective-permute-done.4.refs_1_), channel_id=1, source_target_pairs={{0,2},{2,4},{4,6},{6,8},{8,10},{10,12},{12,14},{14,0},{1,3},{3,5},... | collective-permute-start | bytes 1228808 | tf_op jit(solution)/shard_map/ppermute | solution.py:19
  72.0 15.8 %copy-start.6 = (bf16[2,4,40,640]{3,2,1,0:T(8,128)(2,1)}, bf16[2,4,40,640]{3,2,1,0:T(8,128)(2,1)S(1)}, u32[]{:S(2)}) copy-start(bf16[2,4,40,640]{3,2,1,0:T(8,128)(2,1)S(1)} %collective-permute-done.7.refs_4_) | copy-start | bytes 1228804
  72.0 15.8 %collective-permute-start.9 = (bf16[2,4,40,640]{3,2,1,0:T(8,128)(2,1)S(1)}, bf16[2,4,40,640]{3,2,1,0:T(8,128)(2,1)}, u32[]{:S(2)}, u32[]{:S(2)}) collective-permute-start(bf16[2,4,40,640]{3,2,1,0:T(8,128)(2,1)S(1)} %collective-permute-done.7.refs_4_), channel_id=1, source_target_pairs={{0,14},{2,0},{4,2},{6,4},{8,6},{10,8},{12,10},{14,12},{1,15},{3,1}... | collective-permute-start | bytes 1228808 | tf_op jit(solution)/shard_map/ppermute | solution.py:19
  77.3 15.5 %collective-permute-start.8 = (bf16[2,4,40,640]{3,2,1,0:T(8,128)(2,1)}, bf16[2,4,40,640]{3,2,1,0:T(8,128)(2,1)}, u32[]{:S(2)}, u32[]{:S(2)}) collective-permute-start(bf16[2,4,40,640]{3,2,1,0:T(8,128)(2,1)} %collective-permute-done.6.refs_3_), channel_id=1, source_target_pairs={{0,2},{2,4},{4,6},{6,8},{8,10},{10,12},{12,14},{14,0},{1,3},{3,5},... | collective-permute-start | bytes 1228808 | tf_op jit(solution)/shard_map/ppermute | solution.py:19
  80.3 2.9 %copy-start.1 = (bf16[2,8,40,896]{3,2,1,0:T(8,128)(2,1)}, bf16[2,8,40,896]{3,2,1,0:T(8,128)(2,1)S(1)}, u32[]{:S(2)}) copy-start(bf16[2,8,40,896]{3,2,1,0:T(8,128)(2,1)S(1)} %collective-permute-done.11.refs_8_.refs_9_) | copy-start | bytes 3440644
  81.2 20.0 %collective-permute-start.13 = (bf16[2,4,40,896]{3,2,1,0:T(8,128)(2,1)}, bf16[2,4,40,896]{3,2,1,0:T(8,128)(2,1)}, u32[]{:S(2)}, u32[]{:S(2)}) collective-permute-start(bf16[2,4,40,896]{3,2,1,0:T(8,128)(2,1)} %slice.16), channel_id=1, source_target_pairs={{0,16},{16,32},{32,48},{48,0},{1,17},{17,33},{33,49},{49,1},{2,18}... | collective-permute-start | bytes 1720328 | tf_op jit(solution)/shard_map/ppermute | solution.py:19
  83.1 9.7 %copy-start.2 = (bf16[2,8,40,896]{3,2,1,0:T(8,128)(2,1)}, bf16[2,8,40,896]{3,2,1,0:T(8,128)(2,1)S(1)}, u32[]{:S(2)}) copy-start(bf16[2,8,40,896]{3,2,1,0:T(8,128)(2,1)S(1)} %collective-permute-done.12.refs_9_.refs_10_) | copy-start | bytes 3440644
  83.2 18.0 %collective-permute-start.14 = (bf16[2,4,40,896]{3,2,1,0:T(8,128)(2,1)S(1)}, bf16[2,4,40,896]{3,2,1,0:T(8,128)(2,1)S(1)}, u32[]{:S(2)}, u32[]{:S(2)}) collective-permute-start(bf16[2,4,40,896]{3,2,1,0:T(8,128)(2,1)S(1)} %slice.17), channel_id=1, source_target_pairs={{0,48},{16,0},{32,16},{48,32},{1,49},{17,1},{33,17},{49,33},{2,50}... | collective-permute-start | bytes 1720328 | tf_op jit(solution)/shard_map/ppermute | solution.py:19
  87.8 13.4 %collective-permute-start.10 = (bf16[2,4,40,640]{3,2,1,0:T(8,128)(2,1)}, bf16[2,4,40,640]{3,2,1,0:T(8,128)(2,1)S(1)}, u32[]{:S(2)}, u32[]{:S(2)}) collective-permute-start(bf16[2,4,40,640]{3,2,1,0:T(8,128)(2,1)} %collective-permute-done.9.refs_6_), channel_id=1, source_target_pairs={{0,14},{2,0},{4,2},{6,4},{8,6},{10,8},{12,10},{14,12},{1,15},{3,1}... | collective-permute-start | bytes 1228808 | tf_op jit(solution)/shard_map/ppermute | solution.py:19
  101.2 0.7 copy-start.8
  101.2 0.9 copy-start.7
  110.7 10.3 %collective-permute-start.15 = (bf16[2,320,896]{2,1,0:T(8,128)(2,1)}, bf16[2,320,896]{2,1,0:T(8,128)(2,1)S(1)}, u32[]{:S(2)}, u32[]{:S(2)}) collective-permute-start(bf16[2,320,896]{2,1,0:T(8,128)(2,1)} %get-tuple-element.8), channel_id=1, source_target_pairs={{0,64},{64,0},{1,65},{65,1},{2,66},{66,2},{3,67},{67,3},{4,68},{68... | collective-permute-start | bytes 3440648 | tf_op jit(solution)/shard_map/ppermute | solution.py:19
  122.6 15.6 %collective-permute-start.16 = (bf16[2,80,896]{2,1,0:T(8,128)(2,1)S(1)}, bf16[2,80,896]{2,1,0:T(8,128)(2,1)S(1)}, u32[]{:S(2)}, u32[]{:S(2)}) collective-permute-start(bf16[2,80,896]{2,1,0:T(8,128)(2,1)S(1)} %get-tuple-element.11), channel_id=1, source_target_pairs={{0,256},{128,384},{256,0},{384,128},{1,257},{129,385},{257,1},{385... | collective-permute-start | bytes 860168 | tf_op jit(solution)/shard_map/ppermute | solution.py:19
  129.2 20.4 %collective-permute-start.17 = (bf16[2,80,896]{2,1,0:T(8,128)(2,1)S(1)}, bf16[2,80,896]{2,1,0:T(8,128)(2,1)S(1)}, u32[]{:S(2)}, u32[]{:S(2)}) collective-permute-start(bf16[2,80,896]{2,1,0:T(8,128)(2,1)S(1)} %get-tuple-element.13), channel_id=1, source_target_pairs={{0,128},{128,256},{256,384},{384,0},{1,129},{129,257},{257,385},{3... | collective-permute-start | bytes 860168 | tf_op jit(solution)/shard_map/ppermute | solution.py:19
  131.6 23.9 %collective-permute-start.18 = (bf16[2,80,896]{2,1,0:T(8,128)(2,1)S(1)}, bf16[2,80,896]{2,1,0:T(8,128)(2,1)S(1)}, u32[]{:S(2)}, u32[]{:S(2)}) collective-permute-start(bf16[2,80,896]{2,1,0:T(8,128)(2,1)S(1)} %get-tuple-element.12), channel_id=1, source_target_pairs={{0,384},{128,0},{256,128},{384,256},{1,385},{129,1},{257,129},{385... | collective-permute-start | bytes 860168 | tf_op jit(solution)/shard_map/ppermute | solution.py:19
  173.7 9.1 %collective-permute-start.19 = (bf16[320,896]{1,0:T(8,128)(2,1)S(1)}, bf16[320,896]{1,0:T(8,128)(2,1)S(1)}, u32[]{:S(2)}, u32[]{:S(2)}) collective-permute-start(bf16[320,896]{1,0:T(8,128)(2,1)S(1)} %bitcast.71), channel_id=1, source_target_pairs={{0,64},{64,0},{1,65},{65,1},{2,66},{66,2},{3,67},{67,3},{4,68},{68... | collective-permute-start | bytes 1720328 | tf_op jit(solution)/shard_map/ppermute | solution.py:19
